TPU v7x, 512 devices: a whole 4x4x16 slice. The times are simulated.
512 devices in a mesh: tok: 128 (over y, z, core), head: 4 (over x).
Axes of the slice: x: 4, y: 4, z: 16, core: 2. Of those that a mesh axis runs over, the one named last changes fastest.
Arguments:
- queries: bfloat16 [4, 32768, 256], P('head', 'tok'), may hold values from -5 to 5
- key_vectors: bfloat16 [4, 32768, 256], P('head', 'tok'), may hold values from -5 to 5
- value_vectors: bfloat16 [4, 32768, 256], P('head', 'tok'), may hold values from -8 to 8
- token_rate: float32 [4, 32768], P('head', 'tok'), may hold values from 0.1 to 1
- fast_gate: bfloat16 [4, 512, 256], P('head'), may hold values from -0.375 to 0.375
- fast_up: bfloat16 [4, 512, 256], P('head'), may hold values from -0.375 to 0.375
- fast_down: bfloat16 [4, 512, 256], P('head'), may hold values from -0.25 to 0.25
- attention_gain: float32 [4, 256], P('head'), may hold values from 0.25 to 1.75
- memory_gain: float32 [4, 256], P('head'), may hold values from 0.25 to 1.75
Outputs:
- layer_output: bfloat16 [4, 32768, 256], P('head', 'tok')
All inputs are finite; a program needn't handle non-finite values.
Results may differ from a plain program's by a relative error of at most 0.0065.
Values may be sent and summed in bfloat16 or wider, within the bound.
No kernel may reach another device: no remote copies, remote signals or barrier semaphores. Data moves between devices by JAX's collectives and lax.ppermute only.
A program may use at most 64 MiB of HBM per device.

v0:
```python
import jax
import jax.numpy as jnp
from jax import lax
from jax.sharding import Mesh
from jax.sharding import PartitionSpec as P

BLOCK = 256
HALO = 128
NS_STEPS = 2
TOK = ("y", "zh", "zl", "c")
NEAR = ("y", "zl")
FAR = "zh"
PAIR = "c"
first_coeff = 3.4445
second_coeff = -4.775
third_coefficient = 2.0315
step_size = 1.0
norm_floor = 1e-07
epsilon = 1e-06
masked_score = -1e30


def dot(a, b, dims, precision=None):
    return lax.dot_general(
        a, b, (dims, ((), ())), precision=precision, preferred_element_type=jnp.float32
    )


def outer_halo(keys, values, core):
    count = lax.axis_size(TOK)
    swap = [(i, i + 1) for i in range(1, count - 1, 2)] + [
        (i + 1, i) for i in range(1, count - 1, 2)
    ]
    stacked = jnp.stack([keys, values])
    edge = jnp.where(core == 0, stacked[:, :HALO], stacked[:, -HALO:])
    return lax.ppermute(edge, TOK, swap)


def copies_to(array, axis):
    copies = jnp.broadcast_to(array, (lax.axis_size(axis), *array.shape))
    return lax.all_to_all(copies, axis, split_axis=0, concat_axis=0, tiled=True)


def window_attention(queries, pair_keys, pair_values, outer, core, has_outer):
    head_depth = queries.shape[1]
    start = core * HALO
    width = 2 * BLOCK - HALO
    keys = lax.dynamic_slice_in_dim(pair_keys, start, width, 0)
    values = lax.dynamic_slice_in_dim(pair_values, start, width, 0)
    scale = head_depth ** (-0.5)
    inner = dot(queries, keys, ((1,), (1,))) * scale
    outside = dot(queries, outer[0], ((1,), (1,))) * scale
    outside = jnp.where(has_outer, outside, masked_score)
    highest = jnp.maximum(
        jnp.max(inner, axis=1, keepdims=True), jnp.max(outside, axis=1, keepdims=True)
    )
    inner = jnp.exp(inner - highest)
    outside = jnp.exp(outside - highest)
    total = jnp.sum(inner, axis=1, keepdims=True) + jnp.sum(outside, axis=1, keepdims=True)
    inner = (inner / total).astype(jnp.bfloat16)
    outside = (outside / total).astype(jnp.bfloat16)
    return dot(inner, values, ((1,), (0,))) + dot(outside, outer[1], ((1,), (0,)))


def fast_gradients(keys, scaled, gate_weights, up_weights, down_weights):
    gate_value = dot(keys, gate_weights, ((1,), (1,)))
    up_value = dot(keys, up_weights, ((1,), (1,)))
    squashed = jax.nn.sigmoid(gate_value)
    hidden = (gate_value * squashed * up_value).astype(jnp.bfloat16)
    backward = dot(scaled, down_weights, ((1,), (1,)))
    gate_grad = (backward * up_value * squashed * (1.0 + gate_value * (1.0 - squashed))).astype(
        jnp.bfloat16
    )
    up_grad = (backward * gate_value * squashed).astype(jnp.bfloat16)
    return jnp.concatenate(
        [
            dot(gate_grad, keys, ((0,), (0,))).astype(jnp.bfloat16),
            dot(up_grad, keys, ((0,), (0,))).astype(jnp.bfloat16),
            dot(hidden, scaled, ((0,), (0,))).astype(jnp.bfloat16),
        ],
        axis=1,
    )


def sum_over_tokens(grads):
    near = lax.axis_size(NEAR)
    tiles = grads.reshape(near, -1, grads.shape[1])
    arrived = lax.all_to_all(tiles, NEAR, split_axis=0, concat_axis=0, tiled=True)
    own = jnp.sum(arrived.astype(jnp.float32), axis=0).astype(jnp.bfloat16)
    own = jnp.sum(copies_to(own, FAR).astype(jnp.float32), axis=0).astype(jnp.bfloat16)
    half = copies_to(own, NEAR).reshape(grads.shape)
    return lax.all_gather(half, PAIR, axis=0, tiled=True)


def orthogonalize(grad):
    grad = grad.astype(jnp.float32)
    current = grad * (1.0 / (jnp.sqrt(jnp.sum(grad * grad)) + norm_floor))
    for iteration in range(NS_STEPS):
        product = dot(current, current, ((0,), (0,)), lax.Precision.HIGH)
        squared = dot(product, product, ((1,), (0,)), lax.Precision.HIGH)
        mixer = second_coeff * product + third_coefficient * squared
        current = first_coeff * current + dot(current, mixer, ((1,), (0,)), lax.Precision.HIGH)
    return current


def on_device(
    queries,
    key_vectors,
    value_vectors,
    token_rate,
    fast_gate,
    fast_up,
    fast_down,
    attention_gain,
    memory_gain,
):
    queries, keys, values = (queries[0], key_vectors[0], value_vectors[0])
    rates = token_rate[0]
    head_depth = queries.shape[1]
    hidden_units = fast_gate.shape[1]
    core = lax.axis_index(PAIR)
    index = lax.axis_index(TOK)
    has_outer = jnp.where(core == 0, index > 0, index < lax.axis_size(TOK) - 1)
    scaled = (rates[:, None] * values.astype(jnp.float32)).astype(jnp.bfloat16)
    pair = lax.all_gather(jnp.stack([keys, scaled, values]), PAIR, axis=1, tiled=True)
    half = hidden_units // 2
    mine = [
        lax.dynamic_slice_in_dim(w[0], core * half, half, 0)
        for w in (fast_gate, fast_up, fast_down)
    ]
    grads = fast_gradients(pair[0], pair[1], *mine)
    summed = sum_over_tokens(grads)
    outer = outer_halo(keys, values, core)
    attended = window_attention(queries, pair[0], pair[2], outer, core, has_outer)
    squares = jnp.sum(attended * attended, axis=1)
    width_sum = jnp.sum(copies_to(squares.reshape(1, -1), "head"), axis=0)[0]
    width_mean = width_sum / (lax.axis_size("head") * head_depth)
    attention_part = attended * lax.rsqrt(width_mean + epsilon)[:, None] * attention_gain
    renewed = []
    for i, w in enumerate((fast_gate, fast_up, fast_down)):
        update = orthogonalize(summed[:, i * head_depth : (i + 1) * head_depth])
        renewed.append((w[0].astype(jnp.float32) + step_size * update).astype(jnp.bfloat16))
    gate_value = dot(queries, renewed[0], ((1,), (1,)))
    up_value = dot(queries, renewed[1], ((1,), (1,)))
    memory_hidden = (jax.nn.silu(gate_value) * up_value).astype(jnp.bfloat16)
    memory = dot(memory_hidden, renewed[2], ((1,), (0,)))
    memory_mean = jnp.mean(memory * memory, axis=1, keepdims=True)
    memory_part = memory * lax.rsqrt(memory_mean + epsilon) * memory_gain
    return (attention_part + memory_part).astype(jnp.bfloat16)[None]


def solution(mesh):
    finer = Mesh(
        mesh.devices.reshape(4, 4, 4, 2, mesh.shape["head"]), ("y", "zh", "zl", "c", "head")
    )
    return jax.shard_map(
        on_device,
        mesh=finer,
        in_specs=(
            P("head", TOK, None),
            P("head", TOK, None),
            P("head", TOK, None),
            P("head", TOK),
            P("head", None, None),
            P("head", None, None),
            P("head", None, None),
            P("head", None),
            P("head", None),
        ),
        out_specs=P("head", TOK, None),
        check_vma=False,
    )
```

profile of v0, /device:TPU:1, one launch (start us, length us, event | category | flops | bytes accessed | tf_op | source)
XLA Modules:
  0.0 101.0 jit_solution(8072750087071840205)
XLA Ops:
  0.0 0.7 copy-done.6
  0.7 1.1 %multiply_convert_fusion.3 = bf16[1,256,256]{2,1,0:T(8,128)(2,1)S(1)} fusion(bf16[1,256,256]{2,1,0:T(8,128)(2,1)} %param.11, f32[256]{0:T(256)S(1)} %bitcast.115), kind=kLoop, calls=%fused_computation.82 | loop fusion | flops 196608 | bytes 263168 | tf_op jit(solution)/shard_map/convert_element_type | solution.py:124
  1.9 9.0 %all_gather.6 = bf16[3,512,256]{2,1,0:T(8,128)(2,1)S(1)} all-gather(bf16[3,256,256]{2,1,0:T(8,128)(2,1)S(1)} %pad_maximum_fusion), channel_id=1, replica_groups=mesh['y'=4,'zh'=4,'zl'=4,'c'=2,'head'=4] {'c'}, dimensions={1}, use_global_device_ids=true | all-gather | bytes 1179648 | tf_op jit(solution)/shard_map/all_gather | solution.py:125
  11.1 0.7 copy-done.3
  11.8 0.3 fusion.35
  12.1 0.7 copy-done.4
  13.0 0.4 convolution_convert_fusion.1
  13.4 0.4 convolution_convert_fusion.2
  13.8 0.4 convolution_convert_fusion
  14.2 0.9 copy.16
  15.2 3.6 %all-to-all-start.1 = ((bf16[16,16,768]{2,1,0:T(8,128)(2,1)}), bf16[16,16,768]{2,1,0:T(8,128)(2,1)S(1)}, u32[]{:S(2)}, u32[]{:S(2)}) async-start(bf16[16,16,768]{2,1,0:T(8,128)(2,1)} %bitcast.13), calls=%async_computation.1 | async-start | bytes 786432 | tf_op jit(solution)/shard_map/all_to_all | solution.py:88
  18.8 3.7 %collective-permute-start = (bf16[2,128,256]{2,1,0:T(8,128)(2,1)S(1)}, bf16[2,128,256]{2,1,0:T(8,128)(2,1)S(1)}, u32[]{:S(2)}, u32[]{:S(2)}) collective-permute-start(bf16[2,128,256]{2,1,0:T(8,128)(2,1)S(1)} %slice_select_fusion), channel_id=1, source_target_pairs={{4,8},{12,16},{20,24},{28,32},{36,40},{44,48},{52,56},{60,64},{68,... | collective-permute-start | bytes 393224 | tf_op jit(solution)/shard_map/ppermute | solution.py:36
  22.6 0.3 fusion.86
  22.8 5.5 %collective-permute-done = bf16[2,128,256]{2,1,0:T(8,128)(2,1)S(1)} collective-permute-done((bf16[2,128,256]{2,1,0:T(8,128)(2,1)S(1)}, bf16[2,128,256]{2,1,0:T(8,128)(2,1)S(1)}, u32[]{:S(2)}, u32[]{:S(2)}) %collective-permute-start) | collective-permute-done | bytes 131104 | tf_op jit(solution)/shard_map/ppermute | solution.py:36
  28.7 3.1 %all-to-all-done.1 = bf16[16,16,768]{2,1,0:T(8,128)(2,1)S(1)} async-done(((bf16[16,16,768]{2,1,0:T(8,128)(2,1)}), bf16[16,16,768]{2,1,0:T(8,128)(2,1)S(1)}, u32[]{:S(2)}, u32[]{:S(2)}) %all-to-all-start.1) | async-done | bytes 393248 | tf_op jit(solution)/shard_map/all_to_all | solution.py:88
  31.8 0.6 broadcast_in_dim.24
  32.5 11.5 %all-to-all-start.2 = ((bf16[4,16,768]{2,1,0:T(8,128)(2,1)}), bf16[4,16,768]{2,1,0:T(8,128)(2,1)S(1)}, u32[]{:S(2)}, u32[]{:S(2)}) async-start(bf16[4,16,768]{2,1,0:T(8,128)(2,1)} %broadcast_in_dim.24), calls=%async_computation.2 | async-start | bytes 196608 | tf_op jit(solution)/shard_map/all_to_all | solution.py:41
  44.0 0.3 fusion.51
  44.5 11.4 %all-to-all-done.2 = bf16[4,16,768]{2,1,0:T(8,128)(2,1)S(1)} async-done(((bf16[4,16,768]{2,1,0:T(8,128)(2,1)}), bf16[4,16,768]{2,1,0:T(8,128)(2,1)S(1)}, u32[]{:S(2)}, u32[]{:S(2)}) %all-to-all-start.2) | async-done | bytes 98336 | tf_op jit(solution)/shard_map/all_to_all | solution.py:41
  55.9 0.6 broadcast_in_dim.23
  56.5 4.0 %all-to-all-start = ((f32[4,1,256]{2,1,0:T(1,128)}), f32[4,1,256]{2,1,0:T(1,128)S(1)}, u32[]{:S(2)}, u32[]{:S(2)}) async-start(f32[4,1,256]{2,1,0:T(1,128)} %broadcast_in_dim.23), calls=%async_computation | async-start | bytes 8192 | tf_op jit(solution)/shard_map/all_to_all | solution.py:41
  60.6 4.1 %all-to-all-done = f32[4,1,256]{2,1,0:T(1,128)S(1)} async-done(((f32[4,1,256]{2,1,0:T(1,128)}), f32[4,1,256]{2,1,0:T(1,128)S(1)}, u32[]{:S(2)}, u32[]{:S(2)}) %all-to-all-start) | async-done | bytes 4128 | tf_op jit(solution)/shard_map/all_to_all | solution.py:41
  64.7 0.8 broadcast_in_dim.25
  65.4 5.1 %all-to-all-start.3 = ((bf16[16,16,768]{2,1,0:T(8,128)(2,1)}), bf16[16,16,768]{2,1,0:T(8,128)(2,1)S(1)}, u32[]{:S(2)}, u32[]{:S(2)}) async-start(bf16[16,16,768]{2,1,0:T(8,128)(2,1)} %broadcast_in_dim.25), calls=%async_computation.3 | async-start | bytes 786432 | tf_op jit(solution)/shard_map/all_to_all | solution.py:41
  70.6 9.9 %all-to-all-done.3 = bf16[16,16,768]{2,1,0:T(8,128)(2,1)S(1)} async-done(((bf16[16,16,768]{2,1,0:T(8,128)(2,1)}), bf16[16,16,768]{2,1,0:T(8,128)(2,1)S(1)}, u32[]{:S(2)}, u32[]{:S(2)}) %all-to-all-start.3) | async-done | bytes 393248 | tf_op jit(solution)/shard_map/all_to_all | solution.py:41
  80.5 7.4 %all_gather.7 = bf16[512,768]{1,0:T(8,128)(2,1)S(1)} all-gather(bf16[256,768]{1,0:T(8,128)(2,1)S(1)} %bitcast.114), channel_id=1, replica_groups=mesh['y'=4,'zh'=4,'zl'=4,'c'=2,'head'=4] {'c'}, dimensions={0}, use_global_device_ids=true | all-gather | bytes 1179648 | tf_op jit(solution)/shard_map/all_gather | solution.py:92
  87.9 0.8 fusion.22
  89.5 0.6 fusion.20
  90.1 0.3 fusion.13
  90.4 0.4 convolution_add_fusion.5
  90.7 0.6 fusion.90
  91.4 0.3 fusion.12
  91.6 0.4 fusion.4
  93.0 0.6 fusion.18
  93.6 0.3 fusion.11
  93.8 0.4 convolution_add_fusion.3
  94.2 0.6 fusion.91
  94.8 0.3 fusion.10
  95.1 0.4 fusion.5
  96.3 0.6 fusion.16
  96.9 0.3 fusion.9
  97.2 0.4 convolution_add_fusion.1
  97.6 0.6 fusion.92
  98.2 0.3 fusion.8
  98.5 0.4 fusion.6
  98.9 0.5 multiply_reduce_fusion
  99.6 0.5 copy-done.7
  100.2 0.8 copy.17
  (35 shorter events, 2.0 us)
Async XLA Ops:
  0.0 22.6 %copy-start = (bf16[1,256,256]{2,1,0:T(8,128)(2,1)S(1)}, bf16[1,256,256]{2,1,0:T(8,128)(2,1)}, u32[]{:S(2)}) copy-start(bf16[1,256,256]{2,1,0:T(8,128)(2,1)} %param.9) | copy-start | bytes 393220
  0.0 0.7 copy-start.6
  0.7 1.1 %copy-start.1 = (bf16[1,256,256]{2,1,0:T(8,128)(2,1)S(1)}, bf16[1,256,256]{2,1,0:T(8,128)(2,1)}, u32[]{:S(2)}) copy-start(bf16[1,256,256]{2,1,0:T(8,128)(2,1)} %param.11) | copy-start | bytes 393220
  0.7 1.1 %copy-start.5 = (bf16[1,256,256]{2,1,0:T(8,128)(2,1)S(1)}, bf16[1,256,256]{2,1,0:T(8,128)(2,1)}, u32[]{:S(2)}) copy-start(bf16[1,256,256]{2,1,0:T(8,128)(2,1)} %param.10) | copy-start | bytes 393220
  1.9 9.0 %copy-start.2 = (bf16[1,512,256]{2,1,0:T(8,128)(2,1)S(1)}, bf16[1,512,256]{2,1,0:T(8,128)(2,1)}, u32[]{:S(2)}) copy-start(bf16[1,512,256]{2,1,0:T(8,128)(2,1)} %param.13) | copy-start | bytes 786436
  10.9 1.0 copy-start.3
  11.8 0.9 copy-start.4
  15.2 16.6 %all-to-all-start.1 = ((bf16[16,16,768]{2,1,0:T(8,128)(2,1)}), bf16[16,16,768]{2,1,0:T(8,128)(2,1)S(1)}, u32[]{:S(2)}, u32[]{:S(2)}) async-start(bf16[16,16,768]{2,1,0:T(8,128)(2,1)} %bitcast.13), calls=%async_computation.1 | async-start | bytes 786432 | tf_op jit(solution)/shard_map/all_to_all | solution.py:88
  18.8 9.6 %collective-permute-start = (bf16[2,128,256]{2,1,0:T(8,128)(2,1)S(1)}, bf16[2,128,256]{2,1,0:T(8,128)(2,1)S(1)}, u32[]{:S(2)}, u32[]{:S(2)}) collective-permute-start(bf16[2,128,256]{2,1,0:T(8,128)(2,1)S(1)} %slice_select_fusion), channel_id=1, source_target_pairs={{4,8},{12,16},{20,24},{28,32},{36,40},{44,48},{52,56},{60,64},{68,... | collective-permute-start | bytes 393224 | tf_op jit(solution)/shard_map/ppermute | solution.py:36
  32.5 23.4 %all-to-all-start.2 = ((bf16[4,16,768]{2,1,0:T(8,128)(2,1)}), bf16[4,16,768]{2,1,0:T(8,128)(2,1)S(1)}, u32[]{:S(2)}, u32[]{:S(2)}) async-start(bf16[4,16,768]{2,1,0:T(8,128)(2,1)} %broadcast_in_dim.24), calls=%async_computation.2 | async-start | bytes 196608 | tf_op jit(solution)/shard_map/all_to_all | solution.py:41
  56.5 8.2 %all-to-all-start = ((f32[4,1,256]{2,1,0:T(1,128)}), f32[4,1,256]{2,1,0:T(1,128)S(1)}, u32[]{:S(2)}, u32[]{:S(2)}) async-start(f32[4,1,256]{2,1,0:T(1,128)} %broadcast_in_dim.23), calls=%async_computation | async-start | bytes 8192 | tf_op jit(solution)/shard_map/all_to_all | solution.py:41
  65.4 15.0 %all-to-all-start.3 = ((bf16[16,16,768]{2,1,0:T(8,128)(2,1)}), bf16[16,16,768]{2,1,0:T(8,128)(2,1)S(1)}, u32[]{:S(2)}, u32[]{:S(2)}) async-start(bf16[16,16,768]{2,1,0:T(8,128)(2,1)} %broadcast_in_dim.25), calls=%async_computation.3 | async-start | bytes 786432 | tf_op jit(solution)/shard_map/all_to_all | solution.py:41
  98.9 0.7 copy-start.8
  99.4 0.7 copy-start.7
where the time goes:
time: 102 us; the launch traced here: 101 us
  waiting for transfers between devices  34 us (33%)
  starting transfers between devices  27.8 us (27%)
  blocking collectives  16.4 us (16%)
  matrix products  11.4 us (11%)
  local copies, waits for them, and re-layouts  6.51 us (6%)
  between operations  2.55 us (2%)
  other arithmetic  2.41 us (2%)
    all_to_all x3, waiting for transfers between devices, copies_to(): return lax.all_to_all(copies, axis, split_axis=0, concat_axis=0, tiled=True)  25.4 us
    all_to_all x3, starting transfers between devices, copies_to(): return lax.all_to_all(copies, axis, split_axis=0, concat_axis=0, tiled=True)  20.6 us
    dot_general x30, matrix products, dot(): lax.dot_general(a, b, (dims, ((), ())), precision=precision, preferred_el...  11.4 us
    all_gather x1, blocking collectives, on_device(): lax.all_gather(jnp.stack([keys, scaled, values]), PAIR, axis=1, tiled=True)  8.97 us
    all_gather x1, blocking collectives, sum_over_tokens(): return lax.all_gather(half, PAIR, axis=0, tiled=True)  7.42 us
    ppermute x1, waiting for transfers between devices, outer_halo(): return lax.ppermute(edge, TOK, swap)  5.51 us
    ppermute x1, starting transfers between devices, outer_halo(): return lax.ppermute(edge, TOK, swap)  3.7 us
    all_to_all x1, starting transfers between devices, sum_over_tokens(): lax.all_to_all(tiles, NEAR, split_axis=0, concat_axis=0, tiled=True)  3.55 us
  transfers between devices with their start and end apart: 5, of which 5 were waited for; matrix products, arithmetic and copies ran while one was open for 1% of the time, Pallas kernels for 0%

commit v1 on v0

--- a/solution.py
+++ b/solution.py
@@ -122,7 +122,12 @@
     index = lax.axis_index(TOK)
     has_outer = jnp.where(core == 0, index > 0, index < lax.axis_size(TOK) - 1)
     scaled = (rates[:, None] * values.astype(jnp.float32)).astype(jnp.bfloat16)
-    pair = lax.all_gather(jnp.stack([keys, scaled, values]), PAIR, axis=1, tiled=True)
+    pair = jnp.concatenate(
+        lax.all_to_all(
+            jnp.stack([jnp.stack([keys, scaled, values])] * lax.axis_size(PAIR)), PAIR, 0, 0
+        ),
+        axis=1,
+    )
     half = hidden_units // 2
     mine = [
         lax.dynamic_slice_in_dim(w[0], core * half, half, 0)

time: 102 us -> 107 us (1.049)
  starting transfers between devices: 27.8 us -> 38.1 us
  blocking collectives: 16.4 us -> 7.42 us
  waiting for transfers between devices: 34 us -> 35.6 us
    all_to_all x0 -> x1, starting transfers between devices: none -> 10.4 us  [on_device(): lax.all_to_all(jnp.stack([jnp.stack([keys, scaled, values])] * lax.axis_s...]
    all_gather x1 -> x0, blocking collectives: 8.97 us -> none  [on_device(): lax.all_gather(jnp.stack([keys, scaled, values]), PAIR, axis=1, tiled=True)]
    all_to_all x0 -> x1, waiting for transfers between devices: none -> 1.56 us  [on_device(): lax.all_to_all(jnp.stack([jnp.stack([keys, scaled, values])] * lax.axis_s...]
  transfers between devices with their start and end apart: 5 -> 6, of which waited for: 5 -> 6; matrix products, arithmetic and copies ran while one was open for 1% -> 1% of each run, Pallas kernels for 0% -> 0%
where the time goes in v1:
time: 107 us; the launch traced here: 106 us
  starting transfers between devices  38.1 us (36%)
  waiting for transfers between devices  35.6 us (33%)
  matrix products  11.4 us (11%)
  local copies, waits for them, and re-layouts  7.43 us (7%)
  blocking collectives  7.42 us (7%)
  other arithmetic  3.34 us (3%)
  between operations  2.52 us (2%)
    all_to_all x3, waiting for transfers between devices, copies_to(): return lax.all_to_all(copies, axis, split_axis=0, concat_axis=0, tiled=True)  25.4 us
    all_to_all x3, starting transfers between devices, copies_to(): return lax.all_to_all(copies, axis, split_axis=0, concat_axis=0, tiled=True)  20.5 us
    dot_general x30, matrix products, dot(): lax.dot_general(a, b, (dims, ((), ())), precision=precision, preferred_el...  11.4 us
    all_to_all x1, starting transfers between devices, on_device(): lax.all_to_all(jnp.stack([jnp.stack([keys, scaled, values])] * lax.axis_s...  10.4 us
    all_gather x1, blocking collectives, sum_over_tokens(): return lax.all_gather(half, PAIR, axis=0, tiled=True)  7.42 us
    ppermute x1, waiting for transfers between devices, outer_halo(): return lax.ppermute(edge, TOK, swap)  5.58 us
    unnamed x19, local copies, waits for them, and re-layouts  3.69 us
    ppermute x1, starting transfers between devices, outer_halo(): return lax.ppermute(edge, TOK, swap)  3.67 us
  transfers between devices with their start and end apart: 6, of which 6 were waited for; matrix products, arithmetic and copies ran while one was open for 1% of the time, Pallas kernels for 0%

profile of v1, /device:TPU:1, one launch (start us, length us, event | category | flops | bytes accessed | tf_op | source)
XLA Modules:
  0.0 105.8 jit_solution(6411292059007035951)
XLA Ops:
  0.0 0.7 copy-done.6
  0.7 1.1 %multiply_convert_fusion.3 = bf16[1,256,256]{2,1,0:T(8,128)(2,1)S(1)} fusion(bf16[1,256,256]{2,1,0:T(8,128)(2,1)} %param.11, f32[256]{0:T(256)S(1)} %bitcast.115), kind=kLoop, calls=%fused_computation.76 | loop fusion | flops 196608 | bytes 263168 | tf_op jit(solution)/shard_map/convert_element_type | solution.py:124
  1.9 0.9 pad_maximum_fusion
  2.8 10.4 %all-to-all-start = ((bf16[2,3,256,256]{3,2,1,0:T(8,128)(2,1)}), bf16[2,3,256,256]{3,2,1,0:T(8,128)(2,1)S(1)}, u32[]{:S(2)}, u32[]{:S(2)}) async-start(bf16[2,3,256,256]{3,2,1,0:T(8,128)(2,1)} %pad_maximum_fusion), calls=%async_computation | async-start | bytes 1572864 | tf_op jit(solution)/shard_map/all_to_all | solution.py:126
  13.2 1.6 %all-to-all-done = bf16[2,3,256,256]{3,2,1,0:T(8,128)(2,1)S(1)} async-done(((bf16[2,3,256,256]{3,2,1,0:T(8,128)(2,1)}), bf16[2,3,256,256]{3,2,1,0:T(8,128)(2,1)S(1)}, u32[]{:S(2)}, u32[]{:S(2)}) %all-to-all-start) | async-done | bytes 786464 | tf_op jit(solution)/shard_map/all_to_all | solution.py:126
  14.8 0.9 copy-done.2
  15.9 0.7 copy-done.4
  16.9 0.7 copy-done.3
  17.9 0.4 convolution_convert_fusion.1
  18.2 0.4 convolution_convert_fusion.2
  18.7 0.4 convolution_convert_fusion
  19.1 0.9 copy.16
  20.0 3.6 %all-to-all-start.2 = ((bf16[16,16,768]{2,1,0:T(8,128)(2,1)}), bf16[16,16,768]{2,1,0:T(8,128)(2,1)S(1)}, u32[]{:S(2)}, u32[]{:S(2)}) async-start(bf16[16,16,768]{2,1,0:T(8,128)(2,1)} %bitcast.14), calls=%async_computation.2 | async-start | bytes 786432 | tf_op jit(solution)/shard_map/all_to_all | solution.py:88
  23.6 3.7 %collective-permute-start = (bf16[2,128,256]{2,1,0:T(8,128)(2,1)S(1)}, bf16[2,128,256]{2,1,0:T(8,128)(2,1)S(1)}, u32[]{:S(2)}, u32[]{:S(2)}) collective-permute-start(bf16[2,128,256]{2,1,0:T(8,128)(2,1)S(1)} %slice_select_fusion), channel_id=1, source_target_pairs={{4,8},{12,16},{20,24},{28,32},{36,40},{44,48},{52,56},{60,64},{68,... | collective-permute-start | bytes 393224 | tf_op jit(solution)/shard_map/ppermute | solution.py:36
  27.6 5.6 %collective-permute-done = bf16[2,128,256]{2,1,0:T(8,128)(2,1)S(1)} collective-permute-done((bf16[2,128,256]{2,1,0:T(8,128)(2,1)S(1)}, bf16[2,128,256]{2,1,0:T(8,128)(2,1)S(1)}, u32[]{:S(2)}, u32[]{:S(2)}) %collective-permute-start) | collective-permute-done | bytes 131104 | tf_op jit(solution)/shard_map/ppermute | solution.py:36
  33.6 3.1 %all-to-all-done.2 = bf16[16,16,768]{2,1,0:T(8,128)(2,1)S(1)} async-done(((bf16[16,16,768]{2,1,0:T(8,128)(2,1)}), bf16[16,16,768]{2,1,0:T(8,128)(2,1)S(1)}, u32[]{:S(2)}, u32[]{:S(2)}) %all-to-all-start.2) | async-done | bytes 393248 | tf_op jit(solution)/shard_map/all_to_all | solution.py:88
  36.7 0.6 broadcast_in_dim.24
  37.4 11.4 %all-to-all-start.3 = ((bf16[4,16,768]{2,1,0:T(8,128)(2,1)}), bf16[4,16,768]{2,1,0:T(8,128)(2,1)S(1)}, u32[]{:S(2)}, u32[]{:S(2)}) async-start(bf16[4,16,768]{2,1,0:T(8,128)(2,1)} %broadcast_in_dim.24), calls=%async_computation.3 | async-start | bytes 196608 | tf_op jit(solution)/shard_map/all_to_all | solution.py:41
  48.8 0.3 fusion.44
  49.3 11.4 %all-to-all-done.3 = bf16[4,16,768]{2,1,0:T(8,128)(2,1)S(1)} async-done(((bf16[4,16,768]{2,1,0:T(8,128)(2,1)}), bf16[4,16,768]{2,1,0:T(8,128)(2,1)S(1)}, u32[]{:S(2)}, u32[]{:S(2)}) %all-to-all-start.3) | async-done | bytes 98336 | tf_op jit(solution)/shard_map/all_to_all | solution.py:41
  60.8 0.6 broadcast_in_dim.23
  61.4 4.0 %all-to-all-start.1 = ((f32[4,1,256]{2,1,0:T(1,128)}), f32[4,1,256]{2,1,0:T(1,128)S(1)}, u32[]{:S(2)}, u32[]{:S(2)}) async-start(f32[4,1,256]{2,1,0:T(1,128)} %broadcast_in_dim.23), calls=%async_computation.1 | async-start | bytes 8192 | tf_op jit(solution)/shard_map/all_to_all | solution.py:41
  65.4 4.1 %all-to-all-done.1 = f32[4,1,256]{2,1,0:T(1,128)S(1)} async-done(((f32[4,1,256]{2,1,0:T(1,128)}), f32[4,1,256]{2,1,0:T(1,128)S(1)}, u32[]{:S(2)}, u32[]{:S(2)}) %all-to-all-start.1) | async-done | bytes 4128 | tf_op jit(solution)/shard_map/all_to_all | solution.py:41
  69.5 0.8 broadcast_in_dim.25
  70.3 5.1 %all-to-all-start.4 = ((bf16[16,16,768]{2,1,0:T(8,128)(2,1)}), bf16[16,16,768]{2,1,0:T(8,128)(2,1)S(1)}, u32[]{:S(2)}, u32[]{:S(2)}) async-start(bf16[16,16,768]{2,1,0:T(8,128)(2,1)} %broadcast_in_dim.25), calls=%async_computation.4 | async-start | bytes 786432 | tf_op jit(solution)/shard_map/all_to_all | solution.py:41
  75.4 9.9 %all-to-all-done.4 = bf16[16,16,768]{2,1,0:T(8,128)(2,1)S(1)} async-done(((bf16[16,16,768]{2,1,0:T(8,128)(2,1)}), bf16[16,16,768]{2,1,0:T(8,128)(2,1)S(1)}, u32[]{:S(2)}, u32[]{:S(2)}) %all-to-all-start.4) | async-done | bytes 393248 | tf_op jit(solution)/shard_map/all_to_all | solution.py:41
  85.3 7.4 %all_gather.3 = bf16[512,768]{1,0:T(8,128)(2,1)S(1)} all-gather(bf16[256,768]{1,0:T(8,128)(2,1)S(1)} %bitcast.111), channel_id=1, replica_groups=mesh['y'=4,'zh'=4,'zl'=4,'c'=2,'head'=4] {'c'}, dimensions={0}, use_global_device_ids=true | all-gather | bytes 1179648 | tf_op jit(solution)/shard_map/all_gather | solution.py:92
  92.7 0.8 fusion.22
  95.7 0.6 fusion.20
  96.3 0.3 fusion.13
  96.6 0.4 convolution_add_fusion.5
  97.0 0.6 fusion.80
  97.9 0.4 fusion.4
  98.6 0.6 fusion.16
  99.2 0.3 fusion.9
  99.4 0.4 convolution_add_fusion.1
  99.8 0.6 fusion.82
  100.5 0.3 fusion.8
  100.7 0.4 fusion.6
  101.1 0.6 fusion.18
  101.7 0.3 fusion.11
  102.0 0.4 convolution_add_fusion.3
  102.4 0.6 fusion.81
  103.0 0.3 fusion.10
  103.3 0.4 fusion.5
  103.7 0.5 multiply_reduce_fusion
  104.4 0.5 copy-done.7
  105.1 0.8 copy.17
  (37 shorter events, 2.8 us)
Async XLA Ops:
  0.0 27.3 %copy-start = (bf16[1,256,256]{2,1,0:T(8,128)(2,1)S(1)}, bf16[1,256,256]{2,1,0:T(8,128)(2,1)}, u32[]{:S(2)}) copy-start(bf16[1,256,256]{2,1,0:T(8,128)(2,1)} %param.9) | copy-start | bytes 393220
  0.0 0.7 copy-start.6
  0.7 1.1 %copy-start.1 = (bf16[1,256,256]{2,1,0:T(8,128)(2,1)S(1)}, bf16[1,256,256]{2,1,0:T(8,128)(2,1)}, u32[]{:S(2)}) copy-start(bf16[1,256,256]{2,1,0:T(8,128)(2,1)} %param.11) | copy-start | bytes 393220
  0.7 1.1 %copy-start.5 = (bf16[1,256,256]{2,1,0:T(8,128)(2,1)S(1)}, bf16[1,256,256]{2,1,0:T(8,128)(2,1)}, u32[]{:S(2)}) copy-start(bf16[1,256,256]{2,1,0:T(8,128)(2,1)} %param.10) | copy-start | bytes 393220
  2.8 11.9 %all-to-all-start = ((bf16[2,3,256,256]{3,2,1,0:T(8,128)(2,1)}), bf16[2,3,256,256]{3,2,1,0:T(8,128)(2,1)S(1)}, u32[]{:S(2)}, u32[]{:S(2)}) async-start(bf16[2,3,256,256]{3,2,1,0:T(8,128)(2,1)} %pad_maximum_fusion), calls=%async_computation | async-start | bytes 1572864 | tf_op jit(solution)/shard_map/all_to_all | solution.py:126
  14.7 0.9 copy-start.2
  15.7 0.9 copy-start.4
  16.6 0.9 copy-start.3
  20.0 16.7 %all-to-all-start.2 = ((bf16[16,16,768]{2,1,0:T(8,128)(2,1)}), bf16[16,16,768]{2,1,0:T(8,128)(2,1)S(1)}, u32[]{:S(2)}, u32[]{:S(2)}) async-start(bf16[16,16,768]{2,1,0:T(8,128)(2,1)} %bitcast.14), calls=%async_computation.2 | async-start | bytes 786432 | tf_op jit(solution)/shard_map/all_to_all | solution.py:88
  23.6 9.6 %collective-permute-start = (bf16[2,128,256]{2,1,0:T(8,128)(2,1)S(1)}, bf16[2,128,256]{2,1,0:T(8,128)(2,1)S(1)}, u32[]{:S(2)}, u32[]{:S(2)}) collective-permute-start(bf16[2,128,256]{2,1,0:T(8,128)(2,1)S(1)} %slice_select_fusion), channel_id=1, source_target_pairs={{4,8},{12,16},{20,24},{28,32},{36,40},{44,48},{52,56},{60,64},{68,... | collective-permute-start | bytes 393224 | tf_op jit(solution)/shard_map/ppermute | solution.py:36
  37.4 23.4 %all-to-all-start.3 = ((bf16[4,16,768]{2,1,0:T(8,128)(2,1)}), bf16[4,16,768]{2,1,0:T(8,128)(2,1)S(1)}, u32[]{:S(2)}, u32[]{:S(2)}) async-start(bf16[4,16,768]{2,1,0:T(8,128)(2,1)} %broadcast_in_dim.24), calls=%async_computation.3 | async-start | bytes 196608 | tf_op jit(solution)/shard_map/all_to_all | solution.py:41
  61.4 8.2 %all-to-all-start.1 = ((f32[4,1,256]{2,1,0:T(1,128)}), f32[4,1,256]{2,1,0:T(1,128)S(1)}, u32[]{:S(2)}, u32[]{:S(2)}) async-start(f32[4,1,256]{2,1,0:T(1,128)} %broadcast_in_dim.23), calls=%async_computation.1 | async-start | bytes 8192 | tf_op jit(solution)/shard_map/all_to_all | solution.py:41
  70.3 15.0 %all-to-all-start.4 = ((bf16[16,16,768]{2,1,0:T(8,128)(2,1)}), bf16[16,16,768]{2,1,0:T(8,128)(2,1)S(1)}, u32[]{:S(2)}, u32[]{:S(2)}) async-start(bf16[16,16,768]{2,1,0:T(8,128)(2,1)} %broadcast_in_dim.25), calls=%async_computation.4 | async-start | bytes 786432 | tf_op jit(solution)/shard_map/all_to_all | solution.py:41
  103.7 0.7 copy-start.8
  104.2 0.7 copy-start.7
